TPU v7x, 128 devices: a whole 4x4x4 slice. The times are simulated.
128 devices in a mesh: nodes: 16 (over x_hi, y, core), feat: 8 (over x_lo, z).
Axes of the slice: x: 4 (x_hi: 2, x_lo: 2; x = x_hi * 2 + x_lo), y: 4, z: 4, core: 2. Of those that a mesh axis runs over, the one named last changes fastest.
Arguments:
- feats: bfloat16 [131072, 128], P('nodes', 'feat'), may hold values from -6 to 6
- tiles: bfloat16 [16, 16, 32, 128, 128], P('nodes'), may hold values from -0.25 to 0.25
- dst_block: int32 [16, 16, 32], P('nodes'), may hold values from 0 to 63
- src_block: int32 [16, 16, 32], P('nodes'), may hold values from 0 to 63
- tile_counts: int32 [16, 16], P('nodes'), may hold values from 1 to 32, as said below
- norm: float32 [131072], P('nodes'), may hold values from 0.3 to 3
- weight: bfloat16 [128, 256], P('feat'), may hold values from -0.5 to 0.5
- bias: float32 [256], P('feat'), may hold values from -3 to 3
- cotangent: bfloat16 [131072, 256], P('nodes', 'feat'), may hold values from -6 to 6
Outputs:
- hidden: bfloat16 [131072, 256], P('nodes', 'feat')
- grad_weight: float32 [128, 256], P('feat')
- grad_bias: float32 [256], P('feat')
- grad_feats: float32 [131072, 128], P('nodes', 'feat')
Inputs may be any that keep to these rules, and one draw needn't show every extreme that they name: Slots at or past tile_counts[o, p] hold no tile; one source slab has 32 tiles from every owner slab in every draw.
All inputs are finite; a program needn't handle non-finite values.
Results may differ from a plain program's by a relative error of at most 0.0075.
Values may be sent and summed in bfloat16 or wider, within the bound.
No kernel may reach another device: no remote copies, remote signals or barrier semaphores. Data moves between devices by JAX's collectives and lax.ppermute only.
A program may use at most 128 MiB of HBM per device.

v0:
```python
import jax
import jax.numpy as jnp
from jax import lax
from jax.sharding import PartitionSpec as P


def silu_slope(pre):
    sigma = jax.nn.sigmoid(pre)
    return sigma * (1.0 + pre * (1.0 - sigma))


def on_device(feats, tiles, dst_block, src_block, tile_counts, norm, weight, bias, cotangent):
    highest = lax.Precision.HIGHEST
    rows_dev = feats.shape[0]
    tile_size = tiles.shape[-1]
    block_count = rows_dev // tile_size
    slot_count = tiles.shape[2]
    feat_local = feats.shape[1]
    own_tiles = tiles[0]
    own_dst = dst_block[0]
    own_src = src_block[0]
    own_counts = tile_counts[0]
    block_ids = jnp.arange(block_count, dtype=jnp.int32)
    slot_ids = jnp.arange(slot_count, dtype=jnp.int32)
    usable_slots = (slot_ids[None, :] < own_counts[:, None]).astype(jnp.float32)
    scaled = (norm[:, None] * feats.astype(jnp.float32)).astype(jnp.bfloat16)
    start_sum = jnp.zeros((block_count, tile_size, feat_local), jnp.float32)
    piece = lax.all_gather(scaled, "nodes", axis=0, tiled=True)
    shards = piece.reshape(piece.shape[0] // rows_dev, block_count, tile_size, feat_local)

    def add_one(position, inner):
        shard = lax.dynamic_index_in_dim(shards, position, 0, keepdims=False)
        tile_set = lax.dynamic_index_in_dim(own_tiles, position, 0, keepdims=False)
        sources = lax.dynamic_index_in_dim(own_src, position, 0, keepdims=False)
        targets = lax.dynamic_index_in_dim(own_dst, position, 0, keepdims=False)
        usable = lax.dynamic_index_in_dim(usable_slots, position, 0, keepdims=False)
        picked = shard[sources]
        product = jnp.einsum("cij,cjf->cif", tile_set, picked, preferred_element_type=jnp.float32)
        placing = (targets[:, None] == block_ids[None, :]).astype(jnp.float32) * usable[:, None]
        return inner + jnp.einsum("cb,cif->bif", placing, product, precision=highest)

    summed = lax.fori_loop(0, shards.shape[0], add_one, start_sum)
    aggregated = (norm[:, None] * summed.reshape(rows_dev, feat_local)).astype(jnp.bfloat16)
    partial_pre = jnp.dot(aggregated, weight, preferred_element_type=jnp.float32)
    pre = lax.psum_scatter(partial_pre, "feat", scatter_dimension=1, tiled=True) + bias
    hidden = jax.nn.silu(pre).astype(jnp.bfloat16)
    grad_pre = (cotangent.astype(jnp.float32) * silu_slope(pre)).astype(jnp.bfloat16)
    piece = lax.all_gather(grad_pre, "feat", axis=1, tiled=True)
    projected = lax.dot_general(
        piece, weight, (((1,), (1,)), ((), ())), preferred_element_type=jnp.float32
    )
    block = lax.dot_general(
        aggregated, piece, (((0,), (0,)), ((), ())), preferred_element_type=jnp.float32
    )
    projected, weight_part = (projected, block)
    scale = (rows_dev * lax.axis_size("nodes")) ** (-0.5)
    bias_part = jnp.sum(grad_pre, axis=0, dtype=jnp.float32)
    weight_sum, bias_sum = lax.psum((weight_part, bias_part), "nodes")
    grad_weight = weight_sum * scale
    grad_bias = bias_sum * scale
    back_scaled = (norm[:, None] * projected).astype(jnp.bfloat16)
    back_blocks = back_scaled.reshape(block_count, tile_size, feat_local)
    picked_back = back_blocks[own_dst]
    partial_back = (
        jnp.einsum("pcij,pcif->pcjf", own_tiles, picked_back, preferred_element_type=jnp.float32)
        * usable_slots[:, :, None, None]
    )
    sources = own_src
    placing = (sources[..., None] == block_ids).astype(jnp.float32)
    returned = lax.psum_scatter(
        jnp.einsum("pcb,pcjf->pbjf", placing, partial_back, precision=highest).reshape(
            rows_dev * lax.axis_size("nodes"), feat_local
        ),
        "nodes",
        scatter_dimension=0,
        tiled=True,
    )
    grad_feats = norm[:, None] * returned
    return (hidden, grad_weight, grad_bias, grad_feats)


def solution(mesh):
    return jax.shard_map(
        on_device,
        mesh=mesh,
        in_specs=(
            P("nodes", "feat"),
            P("nodes", None, None, None, None),
            P("nodes", None, None),
            P("nodes", None, None),
            P("nodes", None),
            P("nodes"),
            P("feat", None),
            P("feat"),
            P("nodes", "feat"),
        ),
        out_specs=(P("nodes", "feat"), P("feat", None), P("feat"), P("nodes", "feat")),
        check_vma=False,
    )
```

profile of v0, /device:TPU:0, one launch (start us, length us, event | category | flops | bytes accessed | tf_op | source)
XLA Modules:
  0.0 432.4 jit_solution(2135381942234439921)
XLA Ops:
  9.7 59.0 %all-gather.3.cloned.1.call-done = bf16[131072,16]{0,1:T(8,128)(2,1)} async-done(((bf16[8192,16]{0,1:T(8,128)(2,1)}), bf16[131072,16]{0,1:T(8,128)(2,1)}) %all-gather.3.cloned.1.call-update) | async-done | bytes 4194320 | tf_op jit(solution)/shard_map/all_gather | solution.py:28
  68.8 4.9 %copy.24 = bf16[2,8,1024,128]{3,2,1,0:T(8,128)(2,1)} copy(bf16[2,8,1024,128]{3,1,2,0:T(8,128)(2,1)} %bitcast.97) | data formatting | bytes 8388608
  73.7 72.4 %while.14 = (s32[]{:T(128)}, f32[64,128,16]{1,0,2:T(8,128)S(1)}, s32[16,32]{1,0:T(8,128)S(1)}, f32[16,32]{1,0:T(8,128)S(1)}, bf16[16,32,128,128]{3,2,1,0:T(8,128...) while((s32[]{:T(128)}, f32[64,128,16]{1,0,2:T(8,128)S(1)}, ...), condition=%wide.region_1.2_spmd.clone, body=%wide.region_0.1_spmd.clone.sunk | while | flops 67376224 | bytes 4068739 | solution.py:42
  75.6 1.9 fusion.54
  80.1 1.9 fusion.54
  84.6 1.9 fusion.54
  89.1 1.9 fusion.54
  93.7 1.9 fusion.54
  98.2 1.9 fusion.54
  102.7 1.9 fusion.54
  107.2 1.9 fusion.54
  111.8 1.9 fusion.54
  116.3 1.9 fusion.54
  120.8 1.9 fusion.54
  125.4 1.9 fusion.54
  129.9 1.9 fusion.54
  134.4 1.9 fusion.54
  138.9 1.9 fusion.54
  143.5 1.9 fusion.54
  146.2 4.5 %fusion.28 = f32[8192,256]{0,1:T(8,128)} fusion(bf16[16,256]{1,0:T(8,128)(2,1)S(1)} %copy-done, f32[2,8,64,128]{3,2,1,0:T(8,128)S(1)} %bitcast.94, f32[8192]{0:T(1024)S(1)} %copy-done.2), kind=kOutput, calls=%fused_computation.48 | convolution fusion | flops 67371008 | bytes 8953856 | tf_op jit(solution)/shard_map/dot_general | solution.py:44
  150.7 90.9 %reduce-scatter.3.cloned.1.call-done = f32[8192,32]{0,1:T(8,128)} async-done(((f32[8192,256]{0,1:T(8,128)}), f32[8192,32]{0,1:T(8,128)}) %reduce-scatter.3.cloned.1.call-update) | async-done | bytes 1048592 | tf_op jit(solution)/shard_map/reduce_scatter | solution.py:45
  241.6 2.9 convert_reduce_fusion
  244.7 51.5 %all-gather.5.cloned.1.call-done = bf16[8192,256]{0,1:T(8,128)(2,1)} async-done(((bf16[8192,32]{0,1:T(8,128)(2,1)}), bf16[8192,256]{0,1:T(8,128)(2,1)}) %all-gather.5.cloned.1.call-update) | async-done | bytes 4194320 | tf_op jit(solution)/shard_map/all_gather | solution.py:48
  296.2 2.8 fusion.21
  299.1 2.0 gather_fusion.1
  301.1 8.4 %fusion.31 = f32[16,32,16,128]{3,2,1,0:T(8,128)S(1)} fusion(bf16[16,32,128,16]{2,3,1,0:T(8,128)(2,1)S(1)} %bitcast.88, bf16[1,16,32,128,128]{4,3,2,1,0:T(8,128)(2,1)} %bitcast.91), kind=kOutput, calls=%fused_computation.55 | convolution fusion | flops 268435456 | bytes 23068672 | tf_op jit(solution)/shard_map/pcij,pcif->pcjf/dot_general | solution.py:65
  309.6 5.0 %fusion.18 = f32[16,64,128,16]{2,1,0,3:T(8,128)S(1)} fusion(s32[16,32]{1,0:T(8,128)S(1)} %get-tuple-element.291, f32[16,32,16,128]{3,2,1,0:T(8,128)S(1)} %fusion.31, f32[16,32]{1,0:T(8,128)S(1)} %get-tuple-element.290), kind=kOutput, calls=%fused_computation.30 | convolution fusion | flops 806387712 | bytes 12587008 | tf_op jit(solution)/shard_map/pcb,pcjf->pbjf/dot_general | solution.py:71
  314.6 8.1 %copy.43 = f32[2,8,1024,128]{3,1,2,0:T(8,128)} copy(f32[2,8,1024,128]{3,2,1,0:T(8,128)S(1)} %bitcast.93) | data formatting | bytes 16777216
  322.7 3.4 fusion.26
  326.1 69.7 %all-reduce = (f32[16,256]{1,0:T(8,128)S(1)}, f32[32]{0:T(128)S(1)}) all-reduce(f32[16,256]{1,0:T(8,128)S(1)} %fusion.26, f32[32]{0:T(128)S(1)} %get-tuple-element.200), channel_id=1, replica_groups=mesh['nodes'=16,'feat'=8] {'nodes'}, use_global_device_ids=true, to_apply=%region_3.4 | all-reduce | flops 4128 | bytes 33024 | tf_op jit(solution)/shard_map/psum | solution.py:58
  397.0 27.0 %reduce-scatter.5.cloned.1.call-done = f32[8192,16]{0,1:T(8,128)} async-done(((f32[131072,16]{0,1:T(8,128)}), f32[8192,16]{0,1:T(8,128)}) %reduce-scatter.5.cloned.1.call-update) | async-done | bytes 524304 | tf_op jit(solution)/shard_map/reduce_scatter | solution.py:70
  424.0 1.9 broadcast_multiply_fusion
  (159 shorter events, 45.5 us)
Async XLA Ops:
  7.2 139.0 %copy-start = (bf16[16,256]{1,0:T(8,128)(2,1)S(1)}, bf16[16,256]{1,0:T(8,128)(2,1)}, u32[]{:S(2)}) copy-start(bf16[16,256]{1,0:T(8,128)(2,1)} %param.17) | copy-start | bytes 24580
  7.2 61.6 %all-gather.3.cloned.1.call-start = ((), (), s32[]{:S(2)}) async-start(), calls=%async_computation.2 | async-start | bytes 4456448 | tf_op jit(solution)/shard_map/all_gather | solution.py:28
  9.0 232.7 %reduce-scatter.3.cloned.1.call-start = ((), (), s32[]{:S(2)}) async-start(), calls=%async_computation.3 | async-start | bytes 9437184 | tf_op jit(solution)/shard_map/reduce_scatter | solution.py:45
  68.8 4.9 %copy-start.4 = (s32[1,16,32]{2,1,0:T(8,128)S(1)}, s32[1,16,32]{2,1,0:T(8,128)}, u32[]{:S(2)}) copy-start(s32[1,16,32]{2,1,0:T(8,128)} %param.14) | copy-start | bytes 6148
  68.8 4.9 %copy-start.5 = (s32[1,16,32]{2,1,0:T(8,128)S(1)}, s32[1,16,32]{2,1,0:T(8,128)}, u32[]{:S(2)}) copy-start(s32[1,16,32]{2,1,0:T(8,128)} %param.13) | copy-start | bytes 6148
  73.7 72.4 %copy-start.2 = (f32[8192]{0:T(1024)S(1)}, f32[8192]{0:T(1024)}, u32[]{:S(2)}) copy-start(f32[8192]{0:T(1024)} %param.16) | copy-start | bytes 98308
  150.7 91.0 %copy-start.3 = (bf16[8192,32]{0,1:T(8,128)(2,1)S(1)}, bf16[8192,32]{0,1:T(8,128)(2,1)}, u32[]{:S(2)}) copy-start(bf16[8192,32]{0,1:T(8,128)(2,1)} %param.19) | copy-start | bytes 1572868
  150.7 91.0 %copy-start.6 = (f32[32]{0:T(128)S(1)}, f32[32]{0:T(128)}, u32[]{:S(2)}) copy-start(f32[32]{0:T(128)} %param.18) | copy-start | bytes 388
  150.7 145.5 %all-gather.5.cloned.1.call-start = ((), (), s32[]{:S(2)}) async-start(), calls=%async_computation.4 | async-start | bytes 4718592 | tf_op jit(solution)/shard_map/all_gather | solution.py:48
  244.5 179.4 %reduce-scatter.5.cloned.1.call-start = ((), (), s32[]{:S(2)}) async-start(), calls=%async_computation.5 | async-start | bytes 8912896 | tf_op jit(solution)/shard_map/reduce_scatter | solution.py:70
  322.7 103.2 %copy-start.1 = (bf16[16,256]{1,0:T(8,128)(2,1)S(1)}, bf16[16,256]{1,0:T(8,128)(2,1)}, u32[]{:S(2)}) copy-start(bf16[16,256]{1,0:T(8,128)(2,1)} %param.17) | copy-start | bytes 24580
Sparse Core Ops, SparseCore 0:
  11.1 57.6 all-gather.2
  150.8 90.7 reduce-scatter.2
  244.7 51.4 all-gather.4
  322.8 101.1 reduce-scatter.4
where the time goes:
time: 434 us; the launch traced here: 432 us
  waiting for transfers between devices  228 us (53%)
  blocking collectives  69.7 us (16%)
  matrix products  67 us (15%)
  local copies, waits for them, and re-layouts  43.6 us (10%)
  between operations  13.9 us (3%)
  other arithmetic  8.6 us (2%)
    reduce_scatter x1, waiting for transfers between devices, on_device(): lax.psum_scatter(partial_pre, 'feat', scatter_dimension=1, tiled=True)  90.9 us
    psum x1, blocking collectives, on_device(): weight_sum, bias_sum = lax.psum((weight_part, bias_part), 'nodes')  69.7 us
    all_gather x1, waiting for transfers between devices, on_device(): piece = lax.all_gather(scaled, 'nodes', axis=0, tiled=True)  59 us
    all_gather x1, waiting for transfers between devices, on_device(): piece = lax.all_gather(grad_pre, 'feat', axis=1, tiled=True)  51.5 us
    dot_general x16, matrix products, add_one(): jnp.einsum('cij,cjf->cif', tile_set, picked, preferred_element_type=jnp.f...  29.8 us
    reduce_scatter x1, waiting for transfers between devices, on_device(): lax.psum_scatter(jnp.einsum('pcb,pcjf->pbjf', placing, partial_back, prec...  27 us
    dynamic_slice x32, local copies, waits for them, and re-layouts, add_one(): shard = lax.dynamic_index_in_dim(shards, position, 0, keepdims=False)  18.5 us
    unnamed x16, local copies, waits for them, and re-layouts  13 us
  transfers between devices with their start and end apart: 4, of which 4 were waited for; matrix products, arithmetic and copies ran while one was open for 1% of the time, Pallas kernels for 0%

commit v1 on v0

--- a/solution.py
+++ b/solution.py
@@ -25,7 +25,9 @@
     usable_slots = (slot_ids[None, :] < own_counts[:, None]).astype(jnp.float32)
     scaled = (norm[:, None] * feats.astype(jnp.float32)).astype(jnp.bfloat16)
     start_sum = jnp.zeros((block_count, tile_size, feat_local), jnp.float32)
-    piece = lax.all_gather(scaled, "nodes", axis=0, tiled=True)
+    piece = jnp.concatenate(
+        lax.all_to_all(jnp.stack([scaled] * lax.axis_size("nodes")), "nodes", 0, 0), axis=0
+    )
     shards = piece.reshape(piece.shape[0] // rows_dev, block_count, tile_size, feat_local)
 
     def add_one(position, inner):

time: 434 us -> 449 us (1.035)
  starting transfers between devices: 0.16 us -> 7.42 us
  waiting for transfers between devices: 228 us -> 235 us
    all_gather x1 -> x0, waiting for transfers between devices: 59 us -> none  [on_device(): piece = lax.all_gather(scaled, 'nodes', axis=0, tiled=True)]
    all_to_all x0 -> x1, waiting for transfers between devices: none -> 55.4 us  [on_device(): lax.all_to_all(jnp.stack([scaled] * lax.axis_size('nodes')), 'nodes', 0, 0)]
    reduce_scatter x1, waiting for transfers between devices: 90.9 us -> 101 us  [on_device(): lax.psum_scatter(partial_pre, 'feat', scatter_dimension=1, tiled=True)]
    all_to_all x0 -> x1, starting transfers between devices: none -> 7.3 us  [on_device(): lax.all_to_all(jnp.stack([scaled] * lax.axis_size('nodes')), 'nodes', 0, 0)]
    unnamed x16 -> x18, local copies, waits for them, and re-layouts: 13 us -> 13.5 us
where the time goes in v1:
time: 449 us; the launch traced here: 448 us
  waiting for transfers between devices  235 us (52%)
  blocking collectives  69.7 us (16%)
  matrix products  67 us (15%)
  local copies, waits for them, and re-layouts  46.4 us (10%)
  between operations  13.9 us (3%)
  starting transfers between devices  7.42 us (2%)
  other arithmetic  7.25 us (2%)
    reduce_scatter x1, waiting for transfers between devices, on_device(): lax.psum_scatter(partial_pre, 'feat', scatter_dimension=1, tiled=True)  101 us
    psum x1, blocking collectives, on_device(): weight_sum, bias_sum = lax.psum((weight_part, bias_part), 'nodes')  69.7 us
    all_to_all x1, waiting for transfers between devices, on_device(): lax.all_to_all(jnp.stack([scaled] * lax.axis_size('nodes')), 'nodes', 0, 0)  55.4 us
    all_gather x1, waiting for transfers between devices, on_device(): piece = lax.all_gather(grad_pre, 'feat', axis=1, tiled=True)  51.5 us
    dot_general x16, matrix products, add_one(): jnp.einsum('cij,cjf->cif', tile_set, picked, preferred_element_type=jnp.f...  29.8 us
    reduce_scatter x1, waiting for transfers between devices, on_device(): lax.psum_scatter(jnp.einsum('pcb,pcjf->pbjf', placing, partial_back, prec...  27 us
    dynamic_slice x32, local copies, waits for them, and re-layouts, add_one(): shard = lax.dynamic_index_in_dim(shards, position, 0, keepdims=False)  18.4 us
    unnamed x18, local copies, waits for them, and re-layouts  13.5 us
  transfers between devices with their start and end apart: 4, of which 4 were waited for; matrix products, arithmetic and copies ran while one was open for 1% of the time, Pallas kernels for 0%

profile of v1, /device:TPU:0, one launch (start us, length us, event | category | flops | bytes accessed | tf_op | source)
XLA Modules:
  0.0 447.6 jit_solution(5569428834225058130)
XLA Ops:
  8.2 2.4 stack.2
  10.6 7.3 %all-to-all-start = ((bf16[16,8192,16]{1,2,0:T(8,128)(2,1)}), bf16[16,8192,16]{1,2,0:T(8,128)(2,1)}, u32[]{:S(2)}, u32[]{:S(2)}) async-start(bf16[16,8192,16]{1,2,0:T(8,128)(2,1)} %stack.2), calls=%async_computation | async-start | bytes 8388608 | tf_op jit(solution)/shard_map/all_to_all | solution.py:29
  18.1 55.4 %all-to-all-done = bf16[16,8192,16]{1,2,0:T(8,128)(2,1)} async-done(((bf16[16,8192,16]{1,2,0:T(8,128)(2,1)}), bf16[16,8192,16]{1,2,0:T(8,128)(2,1)}, u32[]{:S(2)}, u32[]{:S(2)}) %all-to-all-start) | async-done | bytes 4194336 | tf_op jit(solution)/shard_map/all_to_all | solution.py:29
  73.5 5.4 %copy.24 = bf16[32,8,64,128]{3,2,1,0:T(8,128)(2,1)} copy(bf16[32,8,64,128]{3,1,2,0:T(8,128)(2,1)} %bitcast.19) | data formatting | bytes 8388608
  78.8 72.4 %while.14 = (s32[]{:T(128)}, f32[64,128,16]{1,0,2:T(8,128)S(1)}, s32[16,32]{1,0:T(8,128)S(1)}, f32[16,32]{1,0:T(8,128)S(1)}, bf16[16,32,128,128]{3,2,1,0:T(8,128...) while((s32[]{:T(128)}, f32[64,128,16]{1,0,2:T(8,128)S(1)}, ...), condition=%wide.region_1.2_spmd.clone, body=%wide.region_0.1_spmd.clone.sunk | while | flops 67376224 | bytes 4068739 | solution.py:44
  80.7 1.9 fusion.54
  85.2 1.9 fusion.54
  89.7 1.9 fusion.54
  94.2 1.9 fusion.54
  98.8 1.9 fusion.54
  103.3 1.9 fusion.54
  107.8 1.9 fusion.54
  112.3 1.9 fusion.54
  116.9 1.9 fusion.54
  121.4 1.9 fusion.54
  125.9 1.9 fusion.54
  130.4 1.9 fusion.54
  135.0 1.9 fusion.54
  139.5 1.9 fusion.54
  151.2 4.5 %fusion.28 = f32[8192,256]{0,1:T(8,128)} fusion(bf16[16,256]{1,0:T(8,128)(2,1)S(1)} %copy-done, f32[2,8,64,128]{3,2,1,0:T(8,128)S(1)} %bitcast.95, f32[8192]{0:T(1024)S(1)} %copy-done.2), kind=kOutput, calls=%fused_computation.48 | convolution fusion | flops 67371008 | bytes 8953856 | tf_op jit(solution)/shard_map/dot_general | solution.py:46
  155.8 101.0 %reduce-scatter.3.cloned.1.call-done = f32[8192,32]{0,1:T(8,128)} async-done(((f32[8192,256]{0,1:T(8,128)}), f32[8192,32]{0,1:T(8,128)}) %reduce-scatter.3.cloned.1.call-update) | async-done | bytes 1048592 | tf_op jit(solution)/shard_map/reduce_scatter | solution.py:47
  256.8 2.9 convert_reduce_fusion
  259.9 51.5 %all-gather.2.cloned.1.call-done = bf16[8192,256]{0,1:T(8,128)(2,1)} async-done(((bf16[8192,32]{0,1:T(8,128)(2,1)}), bf16[8192,256]{0,1:T(8,128)(2,1)}) %all-gather.2.cloned.1.call-update) | async-done | bytes 4194320 | tf_op jit(solution)/shard_map/all_gather | solution.py:50
  311.4 2.8 fusion.21
  314.3 2.0 gather_fusion.1
  316.3 8.4 %fusion.31 = f32[16,32,16,128]{3,2,1,0:T(8,128)S(1)} fusion(bf16[16,32,128,16]{2,3,1,0:T(8,128)(2,1)S(1)} %bitcast.89, bf16[1,16,32,128,128]{4,3,2,1,0:T(8,128)(2,1)} %bitcast.92), kind=kOutput, calls=%fused_computation.55 | convolution fusion | flops 268435456 | bytes 23068672 | tf_op jit(solution)/shard_map/pcij,pcif->pcjf/dot_general | solution.py:67
  324.8 5.0 %fusion.18 = f32[16,64,128,16]{2,1,0,3:T(8,128)S(1)} fusion(s32[16,32]{1,0:T(8,128)S(1)} %get-tuple-element.282, f32[16,32,16,128]{3,2,1,0:T(8,128)S(1)} %fusion.31, f32[16,32]{1,0:T(8,128)S(1)} %get-tuple-element.281), kind=kOutput, calls=%fused_computation.30 | convolution fusion | flops 806387712 | bytes 12587008 | tf_op jit(solution)/shard_map/pcb,pcjf->pbjf/dot_general | solution.py:73
  329.8 8.1 %copy.43 = f32[2,8,1024,128]{3,1,2,0:T(8,128)} copy(f32[2,8,1024,128]{3,2,1,0:T(8,128)S(1)} %bitcast.94) | data formatting | bytes 16777216
  337.9 3.4 fusion.26
  341.3 69.7 %all-reduce = (f32[16,256]{1,0:T(8,128)S(1)}, f32[32]{0:T(128)S(1)}) all-reduce(f32[16,256]{1,0:T(8,128)S(1)} %fusion.26, f32[32]{0:T(128)S(1)} %get-tuple-element.193), channel_id=1, replica_groups=mesh['nodes'=16,'feat'=8] {'nodes'}, use_global_device_ids=true, to_apply=%region_3.4 | all-reduce | flops 4128 | bytes 33024 | tf_op jit(solution)/shard_map/psum | solution.py:60
  412.2 27.0 %reduce-scatter.5.cloned.1.call-done = f32[8192,16]{0,1:T(8,128)} async-done(((f32[131072,16]{0,1:T(8,128)}), f32[8192,16]{0,1:T(8,128)}) %reduce-scatter.5.cloned.1.call-update) | async-done | bytes 524304 | tf_op jit(solution)/shard_map/reduce_scatter | solution.py:72
  439.1 1.9 broadcast_multiply_fusion
  (161 shorter events, 47.8 us)
Async XLA Ops:
  7.2 144.1 %copy-start = (bf16[16,256]{1,0:T(8,128)(2,1)S(1)}, bf16[16,256]{1,0:T(8,128)(2,1)}, u32[]{:S(2)}) copy-start(bf16[16,256]{1,0:T(8,128)(2,1)} %param.17) | copy-start | bytes 24580
  10.6 7.4 %copy-start.7 = (s32[1,16]{1,0:T(1,128)S(1)}, s32[1,16]{1,0:T(1,128)}, u32[]{:S(2)}) copy-start(s32[1,16]{1,0:T(1,128)} %param.15) | copy-start | bytes 196
  10.6 62.8 %all-to-all-start = ((bf16[16,8192,16]{1,2,0:T(8,128)(2,1)}), bf16[16,8192,16]{1,2,0:T(8,128)(2,1)}, u32[]{:S(2)}, u32[]{:S(2)}) async-start(bf16[16,8192,16]{1,2,0:T(8,128)(2,1)} %stack.2), calls=%async_computation | async-start | bytes 8388608 | tf_op jit(solution)/shard_map/all_to_all | solution.py:29
  17.9 238.9 %reduce-scatter.3.cloned.1.call-start = ((), (), s32[]{:S(2)}) async-start(), calls=%async_computation.3 | async-start | bytes 9437184 | tf_op jit(solution)/shard_map/reduce_scatter | solution.py:47
  73.4 5.4 %copy-start.4 = (s32[1,16,32]{2,1,0:T(8,128)S(1)}, s32[1,16,32]{2,1,0:T(8,128)}, u32[]{:S(2)}) copy-start(s32[1,16,32]{2,1,0:T(8,128)} %param.14) | copy-start | bytes 6148
  73.5 5.4 %copy-start.5 = (s32[1,16,32]{2,1,0:T(8,128)S(1)}, s32[1,16,32]{2,1,0:T(8,128)}, u32[]{:S(2)}) copy-start(s32[1,16,32]{2,1,0:T(8,128)} %param.13) | copy-start | bytes 6148
  78.8 72.4 %copy-start.2 = (f32[8192]{0:T(1024)S(1)}, f32[8192]{0:T(1024)}, u32[]{:S(2)}) copy-start(f32[8192]{0:T(1024)} %param.16) | copy-start | bytes 98308
  155.7 101.1 %copy-start.3 = (bf16[8192,32]{0,1:T(8,128)(2,1)S(1)}, bf16[8192,32]{0,1:T(8,128)(2,1)}, u32[]{:S(2)}) copy-start(bf16[8192,32]{0,1:T(8,128)(2,1)} %param.19) | copy-start | bytes 1572868
  155.7 101.1 %copy-start.6 = (f32[32]{0:T(128)S(1)}, f32[32]{0:T(128)}, u32[]{:S(2)}) copy-start(f32[32]{0:T(128)} %param.18) | copy-start | bytes 388
  155.8 155.6 %all-gather.2.cloned.1.call-start = ((), (), s32[]{:S(2)}) async-start(), calls=%async_computation.4 | async-start | bytes 4718592 | tf_op jit(solution)/shard_map/all_gather | solution.py:50
  259.7 179.4 %reduce-scatter.5.cloned.1.call-start = ((), (), s32[]{:S(2)}) async-start(), calls=%async_computation.5 | async-start | bytes 8912896 | tf_op jit(solution)/shard_map/reduce_scatter | solution.py:72
  337.9 103.1 %copy-start.1 = (bf16[16,256]{1,0:T(8,128)(2,1)S(1)}, bf16[16,256]{1,0:T(8,128)(2,1)}, u32[]{:S(2)}) copy-start(bf16[16,256]{1,0:T(8,128)(2,1)} %param.17) | copy-start | bytes 24580
Sparse Core Ops, SparseCore 0:
  155.9 100.8 reduce-scatter.2
  259.9 51.4 all-gather.1
  338.0 101.0 reduce-scatter.4
